TPU v7x, 32 devices: a whole 2x2x4 slice. The times are simulated.
32 devices in a mesh: section: 4 (over x, core), expert: 4 (over z), tensor: 2 (over y).
Axes of the slice: x: 2, y: 2, z: 4, core: 2. Of those that a mesh axis runs over, the one named last changes fastest.
Arguments:
- tokens: bfloat16 [2048, 5120], P(('section', 'expert'), 'tensor'), may hold values from -6 to 6
- norm_gain: float32 [5120], P('tensor'), may hold values from 0.1 to 1.9
- router: bfloat16 [5120, 4], P('tensor'), may hold values from -0.078125 to 0.078125
- expert_ids: int32 [2048, 1], P(('section', 'expert')), may hold values from 0 to 3; in each aligned block of 128 rows (0 to 127, 128 to 255, ...) at most 64 rows name the same one
- gate_proj: bfloat16 [4, 5120, 4096], P('expert', None, ('section', 'tensor')), may hold values from -0.078125 to 0.078125
- up_proj: bfloat16 [4, 5120, 4096], P('expert', None, ('section', 'tensor')), may hold values from -0.078125 to 0.078125
- down_proj: bfloat16 [4, 4096, 5120], P('expert', 'section', 'tensor'), may hold values from -0.09375 to 0.09375
Outputs:
- moe_out: bfloat16 [2048, 5120], P(('section', 'expert'), 'tensor')
Inputs may be any that keep to these rules, and one draw needn't show every extreme that they name: `expert_ids`: within each aligned block of 128 tokens (the tokens of one group of devices along section and expert) no expert is named by more than 64 tokens, a bound that some block reaches.
All inputs are finite; a program needn't handle non-finite values.
Results may differ from a plain program's by a relative error of at most 0.017.
Values may be sent and summed in bfloat16 or wider, within the bound.
A program may use at most 64 MiB of HBM per device.

v0:
```python
import jax
import jax.numpy as jnp
from jax import lax
from jax.sharding import PartitionSpec as P

D = 5120
EPSILON = 1e-05


def slot_table(expert_ids, experts, capacity):
    chosen = expert_ids[:, 0]
    member = (chosen[:, None] == jnp.arange(experts, dtype=jnp.int32)[None, :]).astype(jnp.int32)
    earlier = jnp.cumsum(member, axis=0) - member
    placed = chosen * capacity + jnp.sum(earlier * member, axis=1)
    placing = placed[:, None] == jnp.arange(experts * capacity, dtype=jnp.int32)[None, :]
    return (member, placing)


def normalize(tokens, norm_gain, squares):
    values = tokens.astype(jnp.float32)
    return (values * lax.rsqrt(squares / D + EPSILON) * norm_gain).astype(jnp.bfloat16)


def on_device(tokens, norm_gain, router, expert_ids, gate_proj, up_proj, down_proj):
    row_count = tokens.shape[0]
    experts = router.shape[1]
    capacity = 2 * row_count // experts
    values = tokens.astype(jnp.float32)
    squares = lax.psum(jnp.sum(values * values, axis=1, keepdims=True), "tensor")
    normed = normalize(tokens, norm_gain, squares)
    logits = lax.psum(jnp.dot(normed, router, preferred_element_type=jnp.float32), "tensor")
    member, placing = slot_table(expert_ids, experts, capacity)
    score = jax.nn.sigmoid(jnp.sum(jnp.where(member > 0, logits, jnp.float32(0.0)), axis=1))
    routed = (normed.astype(jnp.float32) * score[:, None]).astype(jnp.bfloat16)
    placing = placing.astype(jnp.bfloat16)
    outgoing = jnp.einsum("tc,td->cd", placing, routed, preferred_element_type=jnp.float32).astype(
        jnp.bfloat16
    )
    arrived = lax.all_to_all(outgoing, "expert", split_axis=0, concat_axis=0, tiled=True)
    gate_cols = gate_proj[0]
    up_cols = up_proj[0]
    down_rows = down_proj[0]
    widened = lax.all_gather(arrived, "tensor", axis=1, tiled=True)
    piece = lax.all_gather(widened, "section", axis=0, tiled=True)
    gate = jnp.dot(piece, gate_cols, preferred_element_type=jnp.float32)
    upper = jnp.dot(piece, up_cols, preferred_element_type=jnp.float32)
    hidden = (jax.nn.silu(gate) * upper).astype(jnp.bfloat16)
    full_hidden = lax.all_gather(hidden, "tensor", axis=1, tiled=True)
    summed = lax.psum_scatter(
        jnp.dot(full_hidden, down_rows, preferred_element_type=jnp.float32),
        "section",
        scatter_dimension=0,
        tiled=True,
    )
    returned = lax.all_to_all(
        summed.astype(jnp.bfloat16), "expert", split_axis=0, concat_axis=0, tiled=True
    )
    result = jnp.einsum("tc,cd->td", placing, returned, preferred_element_type=jnp.float32)
    return result.astype(jnp.bfloat16)


def solution(mesh):
    in_specs = (
        P(("section", "expert"), "tensor"),
        P("tensor"),
        P("tensor", None),
        P(("section", "expert"), None),
        P("expert", None, ("section", "tensor")),
        P("expert", None, ("section", "tensor")),
        P("expert", "section", "tensor"),
    )
    out_specs = P(("section", "expert"), "tensor")
    return jax.shard_map(
        on_device, mesh=mesh, in_specs=in_specs, out_specs=out_specs, check_vma=False
    )
```

profile of v0, /device:TPU:0, one launch (start us, length us, event | category | flops | bytes accessed | tf_op | source)
XLA Modules:
  0.0 360.6 jit_solution(11621119919947402343)
XLA Ops:
  6.5 0.0 copy-start
  6.5 0.0 copy-start.1
  6.5 0.0 copy-start.2
  6.5 0.0 copy-start.3
  6.5 0.0 all-gather.4.cloned.1.call-start
  6.6 1.4 fusion.8
  7.9 5.9 %psum.14 = f32[128,1]{0,1:T(1,128)S(1)} all-reduce(f32[128,1]{0,1:T(1,128)S(1)} %bitcast.37), channel_id=1, replica_groups=mesh['section'=4,'expert'=4,'tensor'=2] {'tensor'}, use_global_device_ids=true, to_apply=%region_3.0 | all-reduce | flops 128 | bytes 1024 | tf_op jit(solution)/shard_map/psum | solution.py:29
  13.8 0.0 copy-done
  13.9 1.5 fusion.12
  15.3 9.4 %psum.15 = f32[128,4]{1,0:T(8,128)S(1)} all-reduce(f32[128,4]{1,0:T(8,128)S(1)} %fusion.12), channel_id=1, replica_groups=mesh['section'=4,'expert'=4,'tensor'=2] {'tensor'}, use_global_device_ids=true, to_apply=%region_4.5 | all-reduce | flops 512 | bytes 4096 | tf_op jit(solution)/shard_map/psum | solution.py:31
  24.7 0.0 copy-done.3
  24.7 0.1 fusion.17
  24.8 0.2 select_reduce_fusion
  25.0 0.2 reduce_window_sum.11
  25.2 0.2 select_reduce_fusion.1
  25.4 0.0 copy-done.1
  25.4 0.0 copy-done.2
  25.4 0.6 convolution_convert_fusion
  26.0 33.1 %all_to_all.24 = bf16[4,64,2560]{2,1,0:T(8,128)(2,1)} all-to-all(bf16[4,64,2560]{2,1,0:T(8,128)(2,1)S(1)} %bitcast.31), channel_id=1, replica_groups=mesh['section'=4,'expert'=4,'tensor'=2] {'expert'}, dimensions={0} | all-to-all | bytes 2621440 | tf_op jit(solution)/shard_map/all_to_all | solution.py:39
  59.1 0.0 all-gather.4.cloned.1.call-update
  59.2 0.0 all-gather.6.cloned.1.call-start
  59.2 37.2 %all-gather.4.cloned.1.call-done = bf16[256,5120]{1,0:T(8,128)(2,1)} async-done(((bf16[256,2560]{1,0:T(8,128)(2,1)}), bf16[256,5120]{1,0:T(8,128)(2,1)}) %all-gather.4.cloned.1.call-update) | async-done | bytes 2621456 | tf_op jit(solution)/shard_map/all_gather | solution.py:43
  96.5 0.0 all-gather.6.cloned.1.call-update
  96.5 0.0 all-gather.8.cloned.1.call-start
  96.5 71.7 %all-gather.6.cloned.1.call-done = bf16[1024,5120]{1,0:T(8,128)(2,1)} async-done(((bf16[256,5120]{1,0:T(8,128)(2,1)}), bf16[1024,5120]{1,0:T(8,128)(2,1)}) %all-gather.6.cloned.1.call-update) | async-done | bytes 10485776 | tf_op jit(solution)/shard_map/all_gather | solution.py:44
  168.2 0.0 copy-start.4
  168.2 9.9 %fusion.2 = f32[1024,512]{1,0:T(8,128)S(1)} fusion(bf16[1024,5120]{1,0:T(8,128)(2,1)} %all-gather.6.cloned.1.call-done, bf16[1,5120,512]{2,1,0:T(8,128)(2,1)} %param.12), kind=kOutput, calls=%fused_computation.2 | convolution fusion | flops 5368709120 | bytes 17825792 | tf_op jit(solution)/shard_map/dot_general | solution.py:46
  178.2 0.0 copy-done.4
  178.2 8.4 %multiply_convert_fusion = bf16[1024,512]{1,0:T(8,128)(2,1)} fusion(f32[1024,512]{1,0:T(8,128)S(1)} %fusion.2, bf16[1024,5120]{1,0:T(8,128)(2,1)S(1)} %copy-done.4, bf16[1,5120,512]{2,1,0:T(8,128)(2,1)} %param.11), kind=kOutput, calls=%fused_computation.8 | convolution fusion | flops 5371854848 | bytes 18874368 | tf_op jit(solution)/shard_map/dot_general | solution.py:45
  186.6 0.0 all-gather.8.cloned.1.call-update
  186.6 0.0 reduce-scatter.2.cloned.1.call-start
  186.7 33.2 %all-gather.8.cloned.1.call-done = bf16[1024,1024]{1,0:T(8,128)(2,1)} async-done(((bf16[1024,512]{1,0:T(8,128)(2,1)}), bf16[1024,1024]{1,0:T(8,128)(2,1)}) %all-gather.8.cloned.1.call-update) | async-done | bytes 2097168 | tf_op jit(solution)/shard_map/all_gather | solution.py:48
  219.9 10.9 %fusion = f32[1024,2560]{1,0:T(8,128)} fusion(bf16[1024,1024]{1,0:T(8,128)(2,1)} %all-gather.8.cloned.1.call-done, bf16[1,1024,2560]{2,1,0:T(8,128)(2,1)} %param.13), kind=kOutput, calls=%fused_computation | convolution fusion | flops 5368709120 | bytes 17825792 | tf_op jit(solution)/shard_map/dot_general | solution.py:50
  230.8 0.0 reduce-scatter.2.cloned.1.call-update
  230.8 84.6 %reduce-scatter.2.cloned.1.call-done = f32[256,2560]{1,0:T(8,128)} async-done(((f32[1024,2560]{1,0:T(8,128)}), f32[256,2560]{1,0:T(8,128)}) %reduce-scatter.2.cloned.1.call-update) | async-done | bytes 2621456 | tf_op jit(solution)/shard_map/reduce_scatter | solution.py:49
  315.4 1.9 convert_element_type.36
  317.3 35.6 %all_to_all.25 = bf16[4,64,2560]{2,1,0:T(8,128)(2,1)S(1)} all-to-all(bf16[4,64,2560]{2,1,0:T(8,128)(2,1)S(1)} %bitcast.33), channel_id=1, replica_groups=mesh['section'=4,'expert'=4,'tensor'=2] {'expert'}, dimensions={0} | all-to-all | bytes 2621440 | tf_op jit(solution)/shard_map/all_to_all | solution.py:55
  352.9 1.2 convolution_convert_fusion.1
  (3 shorter events, 0.0 us)
Async XLA Ops:
  6.5 7.3 %copy-start = (bf16[2560,4]{0,1:T(4,128)(2,1)S(1)}, bf16[2560,4]{0,1:T(4,128)(2,1)}, u32[]{:S(2)}) copy-start(bf16[2560,4]{0,1:T(4,128)(2,1)} %param.9) | copy-start | bytes 61444
  6.5 18.8 %copy-start.1 = (bf16[128,2560]{1,0:T(8,128)(2,1)S(1)}, bf16[128,2560]{1,0:T(8,128)(2,1)}, u32[]{:S(2)}) copy-start(bf16[128,2560]{1,0:T(8,128)(2,1)} %param.7) | copy-start | bytes 1966084
  6.5 18.8 %copy-start.2 = (f32[2560]{0:T(1024)S(1)}, f32[2560]{0:T(1024)}, u32[]{:S(2)}) copy-start(f32[2560]{0:T(1024)} %param.8) | copy-start | bytes 30724
  6.5 18.2 %copy-start.3 = (s32[128,1]{0,1:T(1,128)S(1)}, s32[128,1]{0,1:T(1,128)}, u32[]{:S(2)}) copy-start(s32[128,1]{0,1:T(1,128)} %param.10) | copy-start | bytes 1540
  6.5 89.9 %all-gather.4.cloned.1.call-start = ((), (), s32[]{:S(2)}) async-start(), calls=%async_computation.3 | async-start | bytes 3932160 | tf_op jit(solution)/shard_map/all_gather | solution.py:43
  59.2 109.0 %all-gather.6.cloned.1.call-start = ((), (), s32[]{:S(2)}) async-start(), calls=%async_computation.4 | async-start | bytes 13107200 | tf_op jit(solution)/shard_map/all_gather | solution.py:44
  96.5 123.4 %all-gather.8.cloned.1.call-start = ((), (), s32[]{:S(2)}) async-start(), calls=%async_computation.5 | async-start | bytes 3145728 | tf_op jit(solution)/shard_map/all_gather | solution.py:48
  168.2 10.0 %copy-start.4 = (bf16[1024,5120]{1,0:T(8,128)(2,1)S(1)}, bf16[1024,5120]{1,0:T(8,128)(2,1)}, u32[]{:S(2)}) copy-start(bf16[1024,5120]{1,0:T(8,128)(2,1)} %all-gather.6.cloned.1.call-done) | copy-start | bytes 31457284
  186.6 128.8 %reduce-scatter.2.cloned.1.call-start = ((), (), s32[]{:S(2)}) async-start(), calls=%async_computation.6 | async-start | bytes 13107200 | tf_op jit(solution)/shard_map/reduce_scatter | solution.py:49
Sparse Core Ops, SparseCore 0:
  59.3 37.1 all-gather.3
  98.0 70.1 all-gather.5
  186.8 33.0 all-gather.7
  231.0 84.3 reduce-scatter.1
where the time goes:
time: 361 us
  waiting for transfers between devices  227 us (63%)
  blocking collectives  83.9 us (23%)
  matrix products  32.7 us (9%)
  between operations  13.2 us (4%)
  other arithmetic  3.86 us (1%)
    reduce_scatter x1, waiting for transfers between devices, on_device(): lax.psum_scatter(jnp.dot(full_hidden, down_rows, preferred_element_type=j...  84.6 us
    all_gather x1, waiting for transfers between devices, on_device(): piece = lax.all_gather(widened, 'section', axis=0, tiled=True)  71.7 us
    all_gather x1, waiting for transfers between devices, on_device(): widened = lax.all_gather(arrived, 'tensor', axis=1, tiled=True)  37.2 us
    all_to_all x1, blocking collectives, on_device(): lax.all_to_all(summed.astype(jnp.bfloat16), 'expert', split_axis=0, conca...  35.6 us
    all_gather x1, waiting for transfers between devices, on_device(): full_hidden = lax.all_gather(hidden, 'tensor', axis=1, tiled=True)  33.2 us
    all_to_all x1, blocking collectives, on_device(): lax.all_to_all(outgoing, 'expert', split_axis=0, concat_axis=0, tiled=True)  33.1 us
    dot_general x1, matrix products, on_device(): jnp.dot(full_hidden, down_rows, preferred_element_type=jnp.float32)  10.9 us
    dot_general x1, matrix products, on_device(): upper = jnp.dot(piece, up_cols, preferred_element_type=jnp.float32)  9.94 us
  transfers between devices with their start and end apart: 4, of which 4 were waited for; matrix products, arithmetic and copies ran while one was open for 0% of the time, Pallas kernels for 0%

commit v1 on v0

--- a/solution.py
+++ b/solution.py
@@ -41,7 +41,14 @@
     up_cols = up_proj[0]
     down_rows = down_proj[0]
     widened = lax.all_gather(arrived, "tensor", axis=1, tiled=True)
-    piece = lax.all_gather(widened, "section", axis=0, tiled=True)
+    ring = [widened]
+    for hop in range(3):
+        ring.append(lax.ppermute(ring[-1], "section", [(dev, (dev + 1) % 4) for dev in range(4)]))
+    piece = jnp.roll(
+        jnp.concatenate(ring[::-1], axis=0),
+        (lax.axis_index("section") + 1) * ring[0].shape[0],
+        axis=0,
+    )
     gate = jnp.dot(piece, gate_cols, preferred_element_type=jnp.float32)
     upper = jnp.dot(piece, up_cols, preferred_element_type=jnp.float32)
     hidden = (jax.nn.silu(gate) * upper).astype(jnp.bfloat16)

time: 361 us -> 393 us (1.089)
  waiting for transfers between devices: 227 us -> 249 us
  local copies, waits for them, and re-layouts: 0.02 us -> 11.1 us
    ppermute x0 -> x3, waiting for transfers between devices: none -> 93.9 us  [on_device(): lax.ppermute(ring[-1], 'section', [(dev, (dev + 1) % 4) for dev in range(...]
    all_gather x1 -> x0, waiting for transfers between devices: 71.7 us -> none  [on_device(): piece = lax.all_gather(widened, 'section', axis=0, tiled=True)]
    unnamed x10 -> x19, local copies, waits for them, and re-layouts: 0.02 us -> 11 us
  transfers between devices with their start and end apart: 4 -> 6, of which waited for: 4 -> 6; matrix products, arithmetic and copies ran while one was open for 0% -> 0% of each run, Pallas kernels for 0% -> 0%
where the time goes in v1:
time: 393 us
  waiting for transfers between devices  249 us (63%)
  blocking collectives  83.9 us (21%)
  matrix products  29 us (7%)
  between operations  13.2 us (3%)
  local copies, waits for them, and re-layouts  11.1 us (3%)
  other arithmetic  6.49 us (2%)
    ppermute x3, waiting for transfers between devices, on_device(): lax.ppermute(ring[-1], 'section', [(dev, (dev + 1) % 4) for dev in range(...  93.9 us
    reduce_scatter x1, waiting for transfers between devices, on_device(): lax.psum_scatter(jnp.dot(full_hidden, down_rows, preferred_element_type=j...  84.6 us
    all_gather x1, waiting for transfers between devices, on_device(): widened = lax.all_gather(arrived, 'tensor', axis=1, tiled=True)  37.3 us
    all_to_all x1, blocking collectives, on_device(): lax.all_to_all(summed.astype(jnp.bfloat16), 'expert', split_axis=0, conca...  35.6 us
    all_gather x1, waiting for transfers between devices, on_device(): full_hidden = lax.all_gather(hidden, 'tensor', axis=1, tiled=True)  33.2 us
    all_to_all x1, blocking collectives, on_device(): lax.all_to_all(outgoing, 'expert', split_axis=0, concat_axis=0, tiled=True)  33.1 us
    unnamed x19, local copies, waits for them, and re-layouts  11 us
    dot_general x1, matrix products, on_device(): jnp.dot(full_hidden, down_rows, preferred_element_type=jnp.float32)  10.9 us
  transfers between devices with their start and end apart: 6, of which 6 were waited for; matrix products, arithmetic and copies ran while one was open for 0% of the time, Pallas kernels for 0%

profile of v1, /device:TPU:0, one launch (start us, length us, event | category | flops | bytes accessed | tf_op | source)
XLA Modules:
  0.0 392.8 jit_solution(3552048680546404500)
XLA Ops:
  6.5 0.0 copy-start
  6.5 0.0 copy-start.3
  6.5 0.0 all-gather.3.cloned.1.call-start
  6.5 0.8 fusion.17
  7.4 0.2 reduce_window_sum.11
  7.5 0.8 select_reduce_fusion.1
  8.4 0.7 fusion.18
  9.0 1.3 fusion.8
  10.3 5.9 %psum.14 = f32[128,1]{0,1:T(1,128)S(1)} all-reduce(f32[128,1]{0,1:T(1,128)S(1)} %bitcast.35), channel_id=1, replica_groups=mesh['section'=4,'expert'=4,'tensor'=2] {'tensor'}, use_global_device_ids=true, to_apply=%region_3.0 | all-reduce | flops 128 | bytes 1024 | tf_op jit(solution)/shard_map/psum | solution.py:29
  16.2 0.0 copy-done
  16.2 1.5 fusion.12
  17.7 9.4 %psum.15 = f32[128,4]{1,0:T(8,128)S(1)} all-reduce(f32[128,4]{1,0:T(8,128)S(1)} %fusion.12), channel_id=1, replica_groups=mesh['section'=4,'expert'=4,'tensor'=2] {'tensor'}, use_global_device_ids=true, to_apply=%region_4.5 | all-reduce | flops 512 | bytes 4096 | tf_op jit(solution)/shard_map/psum | solution.py:31
  27.1 0.8 select_reduce_fusion
  27.9 0.0 copy-done.3
  27.9 1.3 convolution_convert_fusion
  29.3 33.1 %all_to_all.24 = bf16[4,64,2560]{2,1,0:T(8,128)(2,1)} all-to-all(bf16[4,64,2560]{2,1,0:T(8,128)(2,1)S(1)} %bitcast.29), channel_id=1, replica_groups=mesh['section'=4,'expert'=4,'tensor'=2] {'expert'}, dimensions={0} | all-to-all | bytes 2621440 | tf_op jit(solution)/shard_map/all_to_all | solution.py:39
  62.4 0.0 all-gather.3.cloned.1.call-update
  62.4 0.0 all-gather.5.cloned.1.call-start
  62.5 37.3 %all-gather.3.cloned.1.call-done = bf16[256,5120]{1,0:T(8,128)(2,1)} async-done(((bf16[256,2560]{1,0:T(8,128)(2,1)}), bf16[256,5120]{1,0:T(8,128)(2,1)}) %all-gather.3.cloned.1.call-update) | async-done | bytes 2621456 | tf_op jit(solution)/shard_map/all_gather | solution.py:43
  99.7 0.0 collective-permute-start
  99.7 31.3 %collective-permute-done = bf16[256,5120]{1,0:T(8,128)(2,1)S(1)} collective-permute-done((bf16[256,5120]{1,0:T(8,128)(2,1)}, bf16[256,5120]{1,0:T(8,128)(2,1)S(1)}, u32[]{:S(2)}, u32[]{:S(2)}) %collective-permute-start) | collective-permute-done | bytes 2621472 | tf_op jit(solution)/shard_map/ppermute | solution.py:46
  131.0 0.0 collective-permute-start.1
  131.0 31.2 %collective-permute-done.1 = bf16[256,5120]{1,0:T(8,128)(2,1)} collective-permute-done((bf16[256,5120]{1,0:T(8,128)(2,1)S(1)}, bf16[256,5120]{1,0:T(8,128)(2,1)}, u32[]{:S(2)}, u32[]{:S(2)}) %collective-permute-start.1) | collective-permute-done | bytes 2621472 | tf_op jit(solution)/shard_map/ppermute | solution.py:46
  162.2 0.0 collective-permute-start.2
  162.2 31.4 %collective-permute-done.2 = bf16[256,5120]{1,0:T(8,128)(2,1)} collective-permute-done((bf16[256,5120]{1,0:T(8,128)(2,1)}, bf16[256,5120]{1,0:T(8,128)(2,1)}, u32[]{:S(2)}, u32[]{:S(2)}) %collective-permute-start.2) | collective-permute-done | bytes 2621472 | tf_op jit(solution)/shard_map/ppermute | solution.py:46
  193.6 1.9 constant_dynamic-update-slice_fusion.7
  195.5 1.9 constant_dynamic-update-slice_fusion.6
  197.4 0.0 copy-start.2
  197.4 0.2 constant_dynamic-update-slice_fusion.5
  197.6 1.6 copy-done.2
  199.1 0.2 constant_dynamic-update-slice_fusion.4
  199.3 1.9 constant_dynamic-update-slice_fusion.3
  201.2 0.0 slice-start
  201.2 2.1 constant_dynamic-update-slice_fusion.2
  203.3 0.0 slice-start.1
  203.3 0.2 constant_dynamic-update-slice_fusion.1
  203.5 0.2 constant_dynamic-update-slice_fusion
  203.7 0.5 slice-done
  204.2 0.6 slice-done.1
  204.8 5.6 %fusion.2 = f32[1024,512]{1,0:T(8,128)S(1)} fusion(bf16[2048,5120]{1,0:T(8,128)(2,1)S(1)} %constant_dynamic-update-slice_fusion, s32[]{:T(128)S(6)} %select_n.19, bf16[1,5120,512]{2,1,0:T(8,128)(2,1)S(1)} %bitcast.37), kind=kOutput, calls=%fused_computation.2 | convolution fusion | flops 5368709120 | bytes 17825796 | tf_op jit(solution)/shard_map/dot_general | solution.py:52
  210.3 8.5 %multiply_convert_fusion = bf16[1024,512]{1,0:T(8,128)(2,1)} fusion(f32[1024,512]{1,0:T(8,128)S(1)} %fusion.2, bf16[1,5120,512]{2,1,0:T(8,128)(2,1)} %param.12, bf16[2048,5120]{1,0:T(8,128)(2,1)S(1)} %constant_dynamic-update-slice_fusion, s32[]{:T(128)S(6)} %select_n.19), kind=kOutput, calls=%fused_computation.10 | convolution fusion | flops 5371854848 | bytes 18874372 | tf_op jit(solution)/shard_map/dot_general | solution.py:53
  218.8 0.0 all-gather.5.cloned.1.call-update
  218.8 0.0 reduce-scatter.2.cloned.1.call-start
  218.9 33.2 %all-gather.5.cloned.1.call-done = bf16[1024,1024]{1,0:T(8,128)(2,1)} async-done(((bf16[1024,512]{1,0:T(8,128)(2,1)}), bf16[1024,1024]{1,0:T(8,128)(2,1)}) %all-gather.5.cloned.1.call-update) | async-done | bytes 2097168 | tf_op jit(solution)/shard_map/all_gather | solution.py:55
  252.1 10.9 %fusion.4 = f32[1024,2560]{1,0:T(8,128)} fusion(bf16[1024,1024]{1,0:T(8,128)(2,1)} %all-gather.5.cloned.1.call-done, bf16[1,1024,2560]{2,1,0:T(8,128)(2,1)} %param.13), kind=kOutput, calls=%fused_computation.4 | convolution fusion | flops 5368709120 | bytes 17825792 | tf_op jit(solution)/shard_map/dot_general | solution.py:57
  263.0 0.0 reduce-scatter.2.cloned.1.call-update
  263.0 84.6 %reduce-scatter.2.cloned.1.call-done = f32[256,2560]{1,0:T(8,128)} async-done(((f32[1024,2560]{1,0:T(8,128)}), f32[256,2560]{1,0:T(8,128)}) %reduce-scatter.2.cloned.1.call-update) | async-done | bytes 2621456 | tf_op jit(solution)/shard_map/reduce_scatter | solution.py:56
  347.6 0.0 copy-start.1
  347.6 1.9 convert_element_type.36
  349.5 35.6 %all_to_all.25 = bf16[4,64,2560]{2,1,0:T(8,128)(2,1)S(1)} all-to-all(bf16[4,64,2560]{2,1,0:T(8,128)(2,1)S(1)} %bitcast.31), channel_id=1, replica_groups=mesh['section'=4,'expert'=4,'tensor'=2] {'expert'}, dimensions={0} | all-to-all | bytes 2621440 | tf_op jit(solution)/shard_map/all_to_all | solution.py:62
  385.0 1.2 convolution_convert_fusion.1
  386.3 0.0 copy-done.1
  (3 shorter events, 0.0 us)
Async XLA Ops:
  6.5 9.7 %copy-start = (bf16[2560,4]{0,1:T(4,128)(2,1)S(1)}, bf16[2560,4]{0,1:T(4,128)(2,1)}, u32[]{:S(2)}) copy-start(bf16[2560,4]{0,1:T(4,128)(2,1)} %param.9) | copy-start | bytes 61444
  6.5 21.4 %copy-start.3 = (bf16[128,2560]{1,0:T(8,128)(2,1)S(1)}, bf16[128,2560]{1,0:T(8,128)(2,1)}, u32[]{:S(2)}) copy-start(bf16[128,2560]{1,0:T(8,128)(2,1)} %param.7) | copy-start | bytes 1966084
  6.5 93.2 %all-gather.3.cloned.1.call-start = ((), (), s32[]{:S(2)}) async-start(), calls=%async_computation.3 | async-start | bytes 3932160 | tf_op jit(solution)/shard_map/all_gather | solution.py:43
  62.4 189.7 %all-gather.5.cloned.1.call-start = ((), (), s32[]{:S(2)}) async-start(), calls=%async_computation.4 | async-start | bytes 3145728 | tf_op jit(solution)/shard_map/all_gather | solution.py:55
  99.7 31.3 %collective-permute-start = (bf16[256,5120]{1,0:T(8,128)(2,1)}, bf16[256,5120]{1,0:T(8,128)(2,1)S(1)}, u32[]{:S(2)}, u32[]{:S(2)}) collective-permute-start(bf16[256,5120]{1,0:T(8,128)(2,1)} %all-gather.3.cloned.1.call-done), channel_id=1, source_target_pairs={{0,8},{8,16},{16,24},{24,0},{1,9},{9,17},{17,25},{25,1},{2,10},{10... | collective-permute-start | bytes 7864328 | tf_op jit(solution)/shard_map/ppermute | solution.py:46
  131.0 31.2 %collective-permute-start.1 = (bf16[256,5120]{1,0:T(8,128)(2,1)S(1)}, bf16[256,5120]{1,0:T(8,128)(2,1)}, u32[]{:S(2)}, u32[]{:S(2)}) collective-permute-start(bf16[256,5120]{1,0:T(8,128)(2,1)S(1)} %collective-permute-done), channel_id=1, source_target_pairs={{0,8},{8,16},{16,24},{24,0},{1,9},{9,17},{17,25},{25,1},{2,10},{10... | collective-permute-start | bytes 7864328 | tf_op jit(solution)/shard_map/ppermute | solution.py:46
  162.2 31.4 %collective-permute-start.2 = (bf16[256,5120]{1,0:T(8,128)(2,1)}, bf16[256,5120]{1,0:T(8,128)(2,1)}, u32[]{:S(2)}, u32[]{:S(2)}) collective-permute-start(bf16[256,5120]{1,0:T(8,128)(2,1)} %collective-permute-done.1), channel_id=1, source_target_pairs={{0,8},{8,16},{16,24},{24,0},{1,9},{9,17},{17,25},{25,1},{2,10},{10... | collective-permute-start | bytes 7864328 | tf_op jit(solution)/shard_map/ppermute | solution.py:46
  197.4 1.7 copy-start.2
  201.2 3.0 slice-start
  203.3 1.5 slice-start.1
  218.8 128.8 %reduce-scatter.2.cloned.1.call-start = ((), (), s32[]{:S(2)}) async-start(), calls=%async_computation.5 | async-start | bytes 13107200 | tf_op jit(solution)/shard_map/reduce_scatter | solution.py:56
  347.6 38.7 %copy-start.1 = (bf16[2560,4]{0,1:T(4,128)(2,1)S(1)}, bf16[2560,4]{0,1:T(4,128)(2,1)}, u32[]{:S(2)}) copy-start(bf16[2560,4]{0,1:T(4,128)(2,1)} %param.9) | copy-start | bytes 61444
Sparse Core Ops, SparseCore 0:
  62.5 37.1 all-gather.2
  218.9 33.0 all-gather.4
  263.2 84.3 reduce-scatter.1
